TPU v7x, 128 devices: a whole 4x4x4 slice. The times are simulated.
128 devices in a mesh: row: 8 (over z_hi, y), col: 16 (over x, z_lo, core).
Axes of the slice: x: 4, y: 4, z: 4 (z_hi: 2, z_lo: 2; z = z_hi * 2 + z_lo), core: 2. Of those that a mesh axis runs over, the one named last changes fastest.
Arguments:
- positions: float32 [3, 16384], P(None, ('row', 'col')), may hold values from 0 to 5
- species: int32 [16384], P(('row', 'col')), may hold values from 0 to 99
- tile_list: int32 [8, 16, 2, 3], P('row', 'col'), may hold values from 0 to 15, as said below
- pair_mask: int32 [8, 16, 2, 128, 128], P('row', 'col'), may hold values 0 or 1
- embed: float32 [100, 128], replicated, may hold values from -6 to 6
- w_in: float32 [2, 128, 128], replicated, may hold values from -0.5 to 0.5
- rbf_weight: bfloat16 [2, 256, 128], replicated, may hold values from -1 to 1
- rbf_bias: float32 [2, 128], replicated, may hold values from -4 to 4
- filt_weight: bfloat16 [2, 128, 128], replicated, may hold values from -1 to 1
- w_update1: float32 [2, 128, 128], replicated, may hold values from -1 to 1
- w_update2: float32 [2, 128, 128], replicated, may hold values from -0.5 to 0.5
- w_out1: float32 [128, 64], replicated, may hold values from -0.5 to 0.5
- w_out2: float32 [64], replicated, may hold values from -0.75 to 0.75
Outputs:
- atom_energy: float32 [16384], P(('row', 'col'))
- forces: float32 [3, 16384], P(None, ('row', 'col'))
Inputs may be any that keep to these rules, and one draw needn't show every extreme that they name: `tile_list`: A live slot (flag 1) names a row block below 16 and a column block below 8; the live slots of one device name distinct row blocks and come first; a dead slot is all zeros; every device has at least one live slot and some device has all 2.
All inputs are finite; a program needn't handle non-finite values. No bound on the sum of `pair_mask` on one device may be relied on, other than what follows from the above.
Results may differ from a plain program's by a relative error of at most 0.007.
Values sent between devices are 32-bit elements; how exact they have to be, the bound alone decides.
No kernel may reach another device: no remote copies, remote signals or barrier semaphores. Data moves between devices by JAX's collectives and lax.ppermute only.
A program may use at most 192 MiB of HBM per device.

v0:
```python
from functools import partial
import math
import jax
import jax.numpy as jnp
from jax import lax
from jax.sharding import PartitionSpec as P

LAYERS = 2
CUTOFF = 5.0
NORM_DIV = 4.0
HIGH = lax.Precision.HIGHEST


def shifted_softplus(values):
    return jax.nn.softplus(values) - math.log(2.0)


def tile_message(row_coord, col_coord, col_feat, pair_gate, rbf_w, rbf_b, filt_w):
    offset = row_coord[:, :, None] - col_coord[:, None, :]
    distance = jnp.sqrt(jnp.sum(offset * offset, axis=0) + 0.01)
    n_gauss = rbf_w.shape[0]
    rows_here = distance.shape[0]
    feat_width = filt_w.shape[1]
    centers = jnp.arange(n_gauss).astype(distance.dtype) * (CUTOFF / n_gauss)
    sharpness = (n_gauss / CUTOFF) ** 2 / 32.0
    expand = jnp.exp(-sharpness * (distance[:, :, None] - centers) ** 2).astype(jnp.bfloat16)
    pre_act = (
        jnp.dot(
            expand.reshape(rows_here * rows_here, n_gauss),
            rbf_w,
            preferred_element_type=jnp.float32,
        )
        + rbf_b
    )
    hidden = shifted_softplus(pre_act).astype(jnp.bfloat16)
    filters = jnp.dot(hidden, filt_w, preferred_element_type=jnp.float32).reshape(
        rows_here, rows_here, feat_width
    )
    envelope = jnp.where(distance < CUTOFF, 0.5 * (jnp.cos(math.pi * distance / CUTOFF) + 1.0), 0.0)
    envelope = envelope * pair_gate.astype(distance.dtype)
    return jnp.einsum("ijf,ij,jf->if", filters, envelope, col_feat) / NORM_DIV


def atom_update(message, w_one, w_two):
    return jnp.dot(shifted_softplus(jnp.dot(message, w_one, precision=HIGH)), w_two, precision=HIGH)


def energy_head(features, w_out1, w_out2):
    return jnp.dot(
        shifted_softplus(jnp.dot(features, w_out1, precision=HIGH)), w_out2, precision=HIGH
    )


def add_rows(target, addend, start, dim_index):
    current = lax.dynamic_slice_in_dim(target, start, addend.shape[dim_index], dim_index)
    return lax.dynamic_update_slice_in_dim(target, current + addend, start, dim_index)


def body(
    positions,
    species,
    tile_list,
    pair_mask,
    embed,
    w_in,
    rbf_weight,
    rbf_bias,
    filt_weight,
    w_update1,
    w_update2,
    w_out1,
    w_out2,
):
    block_len = positions.shape[1]
    feat_width = embed.shape[1]
    slot_count = tile_list.shape[2]
    n_rowdev = lax.axis_size("row")
    n_coldev = lax.axis_size("col")
    table = tile_list.reshape(slot_count, 3)
    gates = pair_mask.reshape(slot_count, block_len, block_len) * table[:, 2][:, None, None]
    row_coords = lax.all_gather(positions, "col", axis=1, tiled=True)
    onehot = (species[:, None] == jnp.arange(embed.shape[0], dtype=jnp.int32)[None, :]).astype(
        jnp.float32
    )
    features = jnp.dot(onehot, embed, precision=HIGH)
    saved = []
    for layer_idx in range(LAYERS):
        mixed_in = jnp.dot(features, w_in[layer_idx], precision=HIGH)
        col_feats, col_coords = (
            lax.all_gather(mixed_in, "row", axis=0, tiled=True),
            lax.all_gather(positions, "row", axis=1, tiled=True),
        )
        partial_sum = jnp.zeros((n_coldev * block_len, feat_width), jnp.float32)
        pullbacks = []
        for slot_idx in range(slot_count):
            row_start = table[slot_idx, 0] * block_len
            col_start = table[slot_idx, 1] * block_len
            row_piece = lax.dynamic_slice_in_dim(row_coords, row_start, block_len, 1)
            col_piece = lax.dynamic_slice_in_dim(col_coords, col_start, block_len, 1)
            feat_piece = lax.dynamic_slice_in_dim(col_feats, col_start, block_len, 0)
            local_fn = partial(
                tile_message,
                pair_gate=gates[slot_idx],
                rbf_w=rbf_weight[layer_idx],
                rbf_b=rbf_bias[layer_idx],
                filt_w=filt_weight[layer_idx],
            )
            message_part = local_fn(row_piece, col_piece, feat_piece)
            partial_sum = add_rows(partial_sum, message_part, row_start, 0)
        message = lax.psum_scatter(partial_sum, "col", scatter_dimension=0, tiled=True)
        update_fn = partial(atom_update, w_one=w_update1[layer_idx], w_two=w_update2[layer_idx])
        update_value, update_pull = jax.vjp(update_fn, message)
        saved.append((col_feats, col_coords, pullbacks, update_pull))
        features = features + update_value

    def head_fn(current_feats):
        return energy_head(current_feats, w_out1, w_out2)

    energies, head_pull = jax.vjp(head_fn, features)
    grad_feat = head_pull(jnp.ones_like(energies))[0]
    row_force = jnp.zeros((3, n_coldev * block_len), jnp.float32)
    col_force = jnp.zeros((3, block_len), jnp.float32)
    for layer_idx in reversed(range(LAYERS)):
        col_feats, col_coords, pullbacks, update_pull = saved[layer_idx]
        grad_msg = update_pull(grad_feat)[0]
        grad_rows = lax.all_gather(grad_msg, "col", axis=0, tiled=True)
        grad_colx = jnp.zeros((n_rowdev * block_len, feat_width), jnp.float32)
        grad_colpos = jnp.zeros((3, n_rowdev * block_len), jnp.float32)
        for slot_idx in range(slot_count):
            row_start = table[slot_idx, 0] * block_len
            col_start = table[slot_idx, 1] * block_len
            cotangent = lax.dynamic_slice_in_dim(grad_rows, row_start, block_len, 0)
            row_piece = lax.dynamic_slice_in_dim(row_coords, row_start, block_len, 1)
            col_piece = lax.dynamic_slice_in_dim(col_coords, col_start, block_len, 1)
            feat_piece = lax.dynamic_slice_in_dim(col_feats, col_start, block_len, 0)
            local_fn = partial(
                tile_message,
                pair_gate=gates[slot_idx],
                rbf_w=rbf_weight[layer_idx],
                rbf_b=rbf_bias[layer_idx],
                filt_w=filt_weight[layer_idx],
            )
            unused_out, pullback = jax.vjp(local_fn, row_piece, col_piece, feat_piece)
            grad_rowp, grad_colp, grad_feats = pullback(cotangent)
            row_force = add_rows(row_force, grad_rowp, row_start, 1)
            grad_colpos = add_rows(grad_colpos, grad_colp, col_start, 1)
            grad_colx = add_rows(grad_colx, grad_feats, col_start, 0)
        grad_inputs, grad_cpos = (
            lax.psum_scatter(grad_colx, "row", scatter_dimension=0, tiled=True),
            lax.psum_scatter(grad_colpos, "row", scatter_dimension=1, tiled=True),
        )
        col_force = col_force + grad_cpos
        grad_feat = grad_feat + jnp.dot(grad_inputs, w_in[layer_idx].T, precision=HIGH)
    own_rows = lax.psum_scatter(row_force, "col", scatter_dimension=1, tiled=True)
    forces = -(own_rows + col_force)
    return (energies, forces)


def solution(mesh):
    return jax.shard_map(
        body,
        mesh=mesh,
        in_specs=(
            P(None, ("row", "col")),
            P(("row", "col")),
            P("row", "col", None, None),
            P("row", "col", None, None, None),
            P(),
            P(),
            P(),
            P(),
            P(),
            P(),
            P(),
            P(),
            P(),
        ),
        out_specs=(P(("row", "col")), P(None, ("row", "col"))),
        check_vma=False,
    )
```

profile of v0, /device:TPU:0, one launch (start us, length us, event | category | flops | bytes accessed | tf_op | source)
XLA Modules:
  0.0 683.8 jit_solution(805372431139413703)
XLA Ops:
  11.1 20.5 %all_gather.19 = f32[3,2048]{1,0:T(4,128)S(1)} all-gather(f32[3,128]{1,0:T(4,128)} %param.15), channel_id=1, replica_groups=mesh['row'=8,'col'=16] {'col'}, dimensions={1}, use_global_device_ids=true | all-gather | bytes 26112 | tf_op jit(solution)/shard_map/all_gather | solution.py:81
  31.6 31.0 %all_gather.20 = f32[3,1024]{1,0:T(4,128)S(1)} all-gather(f32[3,128]{1,0:T(4,128)} %param.15), channel_id=1, replica_groups=mesh['row'=8,'col'=16] {'row'}, dimensions={1}, use_global_device_ids=true | all-gather | bytes 13824 | tf_op jit(solution)/shard_map/all_gather | solution.py:91
  66.2 35.0 %all_gather.21 = f32[1024,128]{1,0:T(8,128)S(1)} all-gather(f32[128,128]{1,0:T(8,128)S(1)} %fusion.108), channel_id=1, replica_groups=mesh['row'=8,'col'=16] {'row'}, dimensions={0}, use_global_device_ids=true | all-gather | bytes 589824 | tf_op jit(solution)/shard_map/all_gather | solution.py:90
  103.2 10.9 %add_convert_fusion.3 = (bf16[16384,128]{1,0:T(8,128)(2,1)S(1)}, f32[16384,128]{1,0:T(8,128)}) fusion(f32[128]{0:T(128)S(1)} %get-tuple-element.65, bf16[2,256,128]{2,1,0:T(8,128)(2,1)} %param.21, f32[256]{0:T(256)S(1)} %convert_multiply_fusion, f32[16384]{0:T(1024)S(1)} %get-tuple-element.54), kind=kOutput, calls=%fused_computation.93 | convolution fusion | flops 1109393408 | bytes 12715520 | tf_op jit(solution)/shard_map/dot_general | solution.py:28
  114.2 6.5 multiply_reduce_fusion.5
  120.7 10.1 %add_convert_fusion.2 = (bf16[16384,128]{1,0:T(8,128)(2,1)S(1)}, f32[16384,128]{1,0:T(8,128)}) fusion(f32[128]{0:T(128)S(1)} %get-tuple-element.65, bf16[2,256,128]{2,1,0:T(8,128)(2,1)S(1)} %copy-done.24, f32[16384]{0:T(1024)S(1)} %get-tuple-element.59, f32[256]{0:T(256)S(1)} %convert_multiply_fusion), kind=kOutput, calls=%fused_computation.90 | convolution fusion | flops 1109393408 | bytes 12715520 | tf_op jit(solution)/shard_map/dot_general | solution.py:28
  130.8 6.4 multiply_reduce_fusion.4
  138.7 11.3 %add_convert_fusion.1 = (bf16[16384,128]{1,0:T(8,128)(2,1)}, f32[16384,128]{1,0:T(8,128)}) fusion(f32[128]{0:T(128)S(1)} %get-tuple-element.64, bf16[2,256,128]{2,1,0:T(8,128)(2,1)S(1)} %copy-done.24, f32[256]{0:T(256)S(1)} %convert_multiply_fusion, f32[16384]{0:T(1024)S(1)} %get-tuple-element.54), kind=kOutput, calls=%fused_computation.89 | convolution fusion | flops 1109393408 | bytes 12715520 | tf_op jit(solution)/shard_map/dot_general | solution.py:28
  150.1 11.4 %add_convert_fusion = (bf16[16384,128]{1,0:T(8,128)(2,1)}, f32[16384,128]{1,0:T(8,128)}) fusion(f32[128]{0:T(128)S(1)} %get-tuple-element.64, bf16[2,256,128]{2,1,0:T(8,128)(2,1)S(1)} %copy-done.24, f32[16384]{0:T(1024)S(1)} %get-tuple-element.59, f32[256]{0:T(256)S(1)} %convert_multiply_fusion), kind=kOutput, calls=%fused_computation.88 | convolution fusion | flops 1109393408 | bytes 12715520 | tf_op jit(solution)/shard_map/dot_general | solution.py:28
  161.5 36.1 %reduce-scatter.10.cloned.1.call-done = f32[128,128]{0,1:T(8,128)} async-done(((f32[2048,128]{0,1:T(8,128)}), f32[128,128]{0,1:T(8,128)}) %reduce-scatter.10.cloned.1.call-update) | async-done | bytes 65552 | tf_op jit(solution)/shard_map/reduce_scatter | solution.py:110
  199.2 35.3 %all_gather.22 = f32[1024,128]{1,0:T(8,128)S(1)} all-gather(f32[128,128]{1,0:T(8,128)S(1)} %fusion.95), channel_id=1, replica_groups=mesh['row'=8,'col'=16] {'row'}, dimensions={0}, use_global_device_ids=true | all-gather | bytes 589824 | tf_op jit(solution)/shard_map/all_gather | solution.py:90
  234.5 6.9 %multiply_reduce_fusion.3 = (f32[128,128]{0,1:T(8,128)S(1)}, f32[128,128,128]{2,1,0:T(8,128)}) fusion(f32[128,128]{0,1:T(8,128)S(1)} %get-tuple-element.43, f32[128,128]{1,0:T(8,128)S(1)} %get-tuple-element.53, bf16[128,128,128]{2,1,0:T(8,128)(2,1)} %bitcast.250, bf16[2,128,128]{2,1,0:T(8,128)(2,1)S(1)} %copy-done.13), kind=kOutput, calls=%fused_computation.85 | convolution fusion | flops 543145984 | bytes 12812288 | tf_op jit(solution)/shard_map/dot_general | solution.py:36
  241.5 6.9 %multiply_reduce_fusion.2 = (f32[128,128]{0,1:T(8,128)S(1)}, f32[128,128,128]{2,1,0:T(8,128)}) fusion(f32[128,128]{0,1:T(8,128)S(1)} %get-tuple-element.42, f32[128,128]{1,0:T(8,128)S(1)} %get-tuple-element.52, bf16[128,128,128]{2,1,0:T(8,128)(2,1)} %bitcast.249, bf16[2,128,128]{2,1,0:T(8,128)(2,1)S(1)} %copy-done.13), kind=kOutput, calls=%fused_computation.84 | convolution fusion | flops 543145984 | bytes 12812288 | tf_op jit(solution)/shard_map/dot_general | solution.py:36
  250.1 60.0 %reduce-scatter.12.cloned.1.call-done = f32[128,128]{0,1:T(8,128)} async-done(((f32[2048,128]{0,1:T(8,128)}), f32[128,128]{0,1:T(8,128)}) %reduce-scatter.12.cloned.1.call-update) | async-done | bytes 65552 | tf_op jit(solution)/shard_map/reduce_scatter | solution.py:110
  313.4 31.0 %all-gather.3.cloned.1.call-done = f32[2048,128]{1,0:T(8,128)} async-done(((f32[128,128]{1,0:T(8,128)}), f32[2048,128]{1,0:T(8,128)}) %all-gather.3.cloned.1.call-update) | async-done | bytes 1048592 | tf_op jit(solution)/shard_map/all_gather | solution.py:126
  345.3 5.2 multiply_reduce_fusion
  350.5 5.2 multiply_reduce_fusion.1
  356.7 71.7 %reduce-scatter.14.cloned.1.call-done = f32[128,128]{1,0:T(8,128)} async-done(((f32[1024,128]{1,0:T(8,128)}), f32[128,128]{1,0:T(8,128)}) %reduce-scatter.14.cloned.1.call-update) | async-done | bytes 65552 | tf_op jit(solution)/shard_map/reduce_scatter | solution.py:149
  430.7 5.6 fusion.49
  436.4 5.7 fusion.48
  442.1 19.9 %all-gather.5.cloned.1.call-done = f32[2048,128]{1,0:T(8,128)} async-done(((f32[128,128]{1,0:T(8,128)}), f32[2048,128]{1,0:T(8,128)}) %all-gather.5.cloned.1.call-update) | async-done | bytes 1048592 | tf_op jit(solution)/shard_map/all_gather | solution.py:126
  462.8 3.1 bitcast_multiply_fusion.6
  465.9 9.3 %fusion.17 = bf16[16384,128]{1,0:T(8,128)(2,1)S(1)} fusion(bf16[16384,128]{1,0:T(8,128)(2,1)S(1)} %bitcast.256, f32[16384,128]{1,0:T(8,128)} %get-tuple-element.79, bf16[2,128,128]{2,1,0:T(8,128)(2,1)S(1)} %copy-done.13), kind=kOutput, calls=%fused_computation.45 | convolution fusion | flops 566231040 | bytes 16809984 | tf_op jit(solution)/shard_map/transpose(jvp())/dot_general | solution.py:36
  475.3 7.1 %fusion.26 = f32[16384]{0:T(1024)S(1)} fusion(f32[256]{0:T(256)S(1)} %convert_multiply_fusion, f32[16384]{0:T(1024)S(1)} %get-tuple-element.54, bf16[16384,128]{1,0:T(8,128)(2,1)S(1)} %fusion.17, bf16[2,256,128]{2,1,0:T(8,128)(2,1)S(1)} %copy-done.24), kind=kOutput, calls=%fused_computation.54 | convolution fusion | flops 1111474176 | bytes 4391936 | tf_op jit(solution)/shard_map/transpose(jvp())/dot_general | solution.py:28
  482.4 7.1 %fusion.21 = bf16[16384,128]{1,0:T(8,128)(2,1)S(1)} fusion(bf16[16384,128]{1,0:T(8,128)(2,1)S(1)} %bitcast.254, f32[16384,128]{1,0:T(8,128)S(1)} %bitcast.264, bf16[2,128,128]{2,1,0:T(8,128)(2,1)S(1)} %copy-done.13), kind=kOutput, calls=%fused_computation.49 | convolution fusion | flops 566231040 | bytes 16809984 | tf_op jit(solution)/shard_map/transpose(jvp())/dot_general | solution.py:36
  489.5 7.3 %fusion.27 = f32[16384]{0:T(1024)S(1)} fusion(f32[256]{0:T(256)S(1)} %convert_multiply_fusion, f32[16384]{0:T(1024)S(1)} %get-tuple-element.54, bf16[16384,128]{1,0:T(8,128)(2,1)S(1)} %fusion.21, bf16[2,256,128]{2,1,0:T(8,128)(2,1)S(1)} %copy-done.24), kind=kOutput, calls=%fused_computation.55 | convolution fusion | flops 1111474176 | bytes 4391936 | tf_op jit(solution)/shard_map/transpose(jvp())/dot_general | solution.py:28
  504.4 9.2 %fusion.23 = bf16[16384,128]{1,0:T(8,128)(2,1)S(1)} fusion(bf16[16384,128]{1,0:T(8,128)(2,1)S(1)} %bitcast.255, f32[16384,128]{1,0:T(8,128)} %get-tuple-element.75, bf16[2,128,128]{2,1,0:T(8,128)(2,1)S(1)} %copy-done.13), kind=kOutput, calls=%fused_computation.51 | convolution fusion | flops 566231040 | bytes 16809984 | tf_op jit(solution)/shard_map/transpose(jvp())/dot_general | solution.py:36
  513.6 7.3 %fusion.25 = f32[16384]{0:T(1024)S(1)} fusion(f32[16384]{0:T(1024)S(1)} %get-tuple-element.59, f32[256]{0:T(256)S(1)} %convert_multiply_fusion, bf16[16384,128]{1,0:T(8,128)(2,1)S(1)} %fusion.23, bf16[2,256,128]{2,1,0:T(8,128)(2,1)S(1)} %copy-done.24), kind=kOutput, calls=%fused_computation.53 | convolution fusion | flops 1111474176 | bytes 4391936 | tf_op jit(solution)/shard_map/transpose(jvp())/dot_general | solution.py:28
  520.9 9.2 %fusion.19 = bf16[16384,128]{1,0:T(8,128)(2,1)S(1)} fusion(bf16[16384,128]{1,0:T(8,128)(2,1)S(1)} %bitcast.253, f32[16384,128]{1,0:T(8,128)} %get-tuple-element.83, bf16[2,128,128]{2,1,0:T(8,128)(2,1)S(1)} %copy-done.13), kind=kOutput, calls=%fused_computation.47 | convolution fusion | flops 566231040 | bytes 16809984 | tf_op jit(solution)/shard_map/transpose(jvp())/dot_general | solution.py:36
  530.2 7.1 %fusion.24 = f32[16384]{0:T(1024)S(1)} fusion(f32[16384]{0:T(1024)S(1)} %get-tuple-element.59, f32[256]{0:T(256)S(1)} %convert_multiply_fusion, bf16[16384,128]{1,0:T(8,128)(2,1)S(1)} %fusion.19, bf16[2,256,128]{2,1,0:T(8,128)(2,1)S(1)} %copy-done.24), kind=kOutput, calls=%fused_computation.52 | convolution fusion | flops 1111474176 | bytes 4391936 | tf_op jit(solution)/shard_map/transpose(jvp())/dot_general | solution.py:28
  541.9 69.4 %reduce-scatter.18.cloned.1.call-done = f32[128,3]{1,0:T(8,128)} async-done(((f32[1024,3]{1,0:T(8,128)}), f32[128,3]{1,0:T(8,128)}) %reduce-scatter.18.cloned.1.call-update) | async-done | bytes 1552
  612.2 62.9 %reduce-scatter.16.cloned.1.call-done = f32[128,3]{1,0:T(8,128)} async-done(((f32[2048,3]{1,0:T(8,128)}), f32[128,3]{1,0:T(8,128)}) %reduce-scatter.16.cloned.1.call-update) | async-done | bytes 1552
  (145 shorter events, 34.3 us)
Async XLA Ops:
  7.2 57.1 %copy-start = (f32[100,128]{1,0:T(8,128)S(1)}, f32[100,128]{1,0:T(8,128)}, u32[]{:S(2)}) copy-start(f32[100,128]{1,0:T(8,128)} %param.19) | copy-start | bytes 153604
  7.2 190.4 %reduce-scatter.10.cloned.1.call-start = ((), (), s32[]{:S(2)}) async-start(), calls=%async_computation.5 | async-start | bytes 1114112 | tf_op jit(solution)/shard_map/reduce_scatter | solution.py:110
  101.2 12.9 %copy-start.16 = (f32[3,128]{1,0:T(4,128)}, f32[3,128]{1,0:T(4,128)S(1)}, u32[]{:S(2)}) copy-start(f32[3,128]{1,0:T(4,128)S(1)} %get-tuple-element.62) | copy-start | bytes 4612
  101.2 12.9 %copy-start.20 = (f32[3,128]{1,0:T(4,128)}, f32[3,128]{1,0:T(4,128)S(1)}, u32[]{:S(2)}) copy-start(f32[3,128]{1,0:T(4,128)S(1)} %get-tuple-element.63) | copy-start | bytes 4612
  101.3 12.8 %copy-start.18 = (f32[3,128]{1,0:T(4,128)}, f32[3,128]{1,0:T(4,128)S(1)}, u32[]{:S(2)}) copy-start(f32[3,128]{1,0:T(4,128)S(1)} %get-tuple-element.60) | copy-start | bytes 4612
  101.3 12.8 %copy-start.22 = (f32[3,128]{1,0:T(4,128)}, f32[3,128]{1,0:T(4,128)S(1)}, u32[]{:S(2)}) copy-start(f32[3,128]{1,0:T(4,128)S(1)} %get-tuple-element.61) | copy-start | bytes 4612
  103.2 10.9 %copy-start.13 = (bf16[2,128,128]{2,1,0:T(8,128)(2,1)S(1)}, bf16[2,128,128]{2,1,0:T(8,128)(2,1)}, u32[]{:S(2)}) copy-start(bf16[2,128,128]{2,1,0:T(8,128)(2,1)} %param.23) | copy-start | bytes 196612
  114.1 6.6 copy-start.24
  138.5 171.7 %reduce-scatter.12.cloned.1.call-start = ((), (), s32[]{:S(2)}) async-start(), calls=%async_computation.6 | async-start | bytes 1114112 | tf_op jit(solution)/shard_map/reduce_scatter | solution.py:110
  150.1 47.5 %copy-start.11 = (f32[2,128,128]{2,1,0:T(8,128)S(1)}, f32[2,128,128]{2,1,0:T(8,128)}, u32[]{:S(2)}) copy-start(f32[2,128,128]{2,1,0:T(8,128)} %param.24) | copy-start | bytes 393220
  150.1 48.7 %copy-start.14 = (f32[2,128,128]{2,1,0:T(8,128)S(1)}, f32[2,128,128]{2,1,0:T(8,128)}, u32[]{:S(2)}) copy-start(f32[2,128,128]{2,1,0:T(8,128)} %param.25) | copy-start | bytes 393220
  150.1 48.9 %copy-start.12 = (f32[2,128,128]{2,1,0:T(8,128)S(1)}, f32[2,128,128]{2,1,0:T(8,128)}, u32[]{:S(2)}) copy-start(f32[2,128,128]{2,1,0:T(8,128)} %param.20) | copy-start | bytes 393220
  241.4 70.1 %copy-start.15 = (f32[128,64]{0,1:T(8,128)S(1)}, f32[128,64]{0,1:T(8,128)}, u32[]{:S(2)}) copy-start(f32[128,64]{0,1:T(8,128)} %param.26) | copy-start | bytes 98308
  241.4 70.4 %copy-start.25 = (f32[64]{0:T(128)S(1)}, f32[64]{0:T(128)}, u32[]{:S(2)}) copy-start(f32[64]{0:T(128)} %param.27) | copy-start | bytes 772
  249.7 94.7 %all-gather.3.cloned.1.call-start = ((), (), s32[]{:S(2)}) async-start(), calls=%async_computation.7 | async-start | bytes 1114112 | tf_op jit(solution)/shard_map/all_gather | solution.py:126
  313.4 115.0 %reduce-scatter.14.cloned.1.call-start = ((), (), s32[]{:S(2)}) async-start(), calls=%async_computation.8 | async-start | bytes 589824 | tf_op jit(solution)/shard_map/reduce_scatter | solution.py:149
  356.7 105.3 %all-gather.5.cloned.1.call-start = ((), (), s32[]{:S(2)}) async-start(), calls=%async_computation.9 | async-start | bytes 1114112 | tf_op jit(solution)/shard_map/all_gather | solution.py:126
  430.7 180.6 %reduce-scatter.18.cloned.1.call-start = ((), (), s32[]{:S(2)}) async-start(), calls=%async_computation.11 | async-start | bytes 589824
  462.8 19.5 %slice-start.4 = ((s8[8388608]{0:T(1024)(128)(4,1)}), s8[4194304]{0:T(1024)(128)(4,1)S(1)}, s32[]{:S(2)}) async-start(s8[8388608]{0:T(1024)(128)(4,1)} %bitcast.263), calls=%async_computation.16 | async-start | bytes 8388608
  465.9 16.5 %slice-start.5 = ((s8[8388608]{0:T(1024)(128)(4,1)}), s8[4194304]{0:T(1024)(128)(4,1)S(1)}, s32[]{:S(2)}) async-start(s8[8388608]{0:T(1024)(128)(4,1)} %bitcast.263), calls=%async_computation.17 | async-start | bytes 8388608
  475.2 21.6 %slice-start = ((s8[8388608]{0:T(1024)(128)(4,1)}), s8[4194304]{0:T(1024)(128)(4,1)S(1)}, s32[]{:S(2)}) async-start(s8[8388608]{0:T(1024)(128)(4,1)} %bitcast.245), calls=%async_computation.12 | async-start | bytes 8388608
  482.4 14.5 %slice-start.1 = ((s8[8388608]{0:T(1024)(128)(4,1)}), s8[4194304]{0:T(1024)(128)(4,1)S(1)}, s32[]{:S(2)}) async-start(s8[8388608]{0:T(1024)(128)(4,1)} %bitcast.245), calls=%async_computation.13 | async-start | bytes 8388608
  496.9 5.2 slice-start.2
  530.1 7.2 %copy-start.6 = (s32[2,128,128]{2,1,0:T(8,128)S(1)}, s32[2,128,128]{2,1,0:T(8,128)}, u32[]{:S(2)}) copy-start(s32[2,128,128]{2,1,0:T(8,128)} %copy-done.5) | copy-start | bytes 393220
  530.1 7.2 %copy-start.8 = (f32[128,128]{1,0:T(8,128)S(1)}, f32[128,128]{1,0:T(8,128)}, u32[]{:S(2)}) copy-start(f32[128,128]{1,0:T(8,128)} %copy-done.7) | copy-start | bytes 196612
  530.2 7.2 %copy-start.10 = (f32[128,128]{1,0:T(8,128)S(1)}, f32[128,128]{1,0:T(8,128)}, u32[]{:S(2)}) copy-start(f32[128,128]{1,0:T(8,128)} %copy-done.9) | copy-start | bytes 196612
  530.2 7.7 %copy-start.21 = (f32[3,128]{1,0:T(4,128)S(1)}, f32[3,128]{1,0:T(4,128)}, u32[]{:S(2)}) copy-start(f32[3,128]{1,0:T(4,128)} %copy-done.20) | copy-start | bytes 4612
  530.2 7.7 %copy-start.23 = (f32[3,128]{1,0:T(4,128)S(1)}, f32[3,128]{1,0:T(4,128)}, u32[]{:S(2)}) copy-start(f32[3,128]{1,0:T(4,128)} %copy-done.22) | copy-start | bytes 4612
  530.2 8.1 %copy-start.17 = (f32[3,128]{1,0:T(4,128)S(1)}, f32[3,128]{1,0:T(4,128)}, u32[]{:S(2)}) copy-start(f32[3,128]{1,0:T(4,128)} %copy-done.16) | copy-start | bytes 4612
  530.2 8.1 %copy-start.19 = (f32[3,128]{1,0:T(4,128)S(1)}, f32[3,128]{1,0:T(4,128)}, u32[]{:S(2)}) copy-start(f32[3,128]{1,0:T(4,128)} %copy-done.18) | copy-start | bytes 4612
  530.2 146.4 %copy-start.1 = (f32[100,128]{1,0:T(8,128)S(1)}, f32[100,128]{1,0:T(8,128)}, u32[]{:S(2)}) copy-start(f32[100,128]{1,0:T(8,128)} %param.19) | copy-start | bytes 153604
  539.7 135.4 %reduce-scatter.16.cloned.1.call-start = ((), (), s32[]{:S(2)}) async-start(), calls=%async_computation.10 | async-start | bytes 1114112
  (7 other events, 9.5 us)
Sparse Core Ops, SparseCore 0:
  138.6 58.9 reduce-scatter.9
  249.8 60.3 reduce-scatter.11
  313.5 30.8 all-gather.2
  356.8 71.5 reduce-scatter.13
  430.8 31.0 all-gather.4
  539.8 71.4 reduce-scatter.17
  613.7 61.3 reduce-scatter.15
where the time goes:
time: 692 us; the launch traced here: 684 us
  waiting for transfers between devices  351 us (51%)
  matrix products  144 us (21%)
  blocking collectives  122 us (18%)
  other arithmetic  37.7 us (5%)
  between operations  17.9 us (3%)
  local copies, waits for them, and re-layouts  10.9 us (2%)
    unnamed x9, waiting for transfers between devices  132 us
    reduce_scatter x2, waiting for transfers between devices, body(): lax.psum_scatter(partial_sum, 'col', scatter_dimension=0, tiled=True)  96.2 us
    dot_general x8, matrix products, tile_message(): jnp.dot(expand.reshape(rows_here * rows_here, n_gauss), rbf_w, preferred_...  72.5 us
    reduce_scatter x1, waiting for transfers between devices, body(): lax.psum_scatter(grad_colx, 'row', scatter_dimension=0, tiled=True)  71.7 us
    all_gather x2, blocking collectives, body(): lax.all_gather(mixed_in, 'row', axis=0, tiled=True)  70.3 us
    dot_general x8, matrix products, tile_message(): jnp.dot(hidden, filt_w, preferred_element_type=jnp.float32)  61.5 us
    all_gather x2, waiting for transfers between devices, body(): grad_rows = lax.all_gather(grad_msg, 'col', axis=0, tiled=True)  50.8 us
    dot_general x8, other arithmetic, tile_message(): return jnp.einsum('ijf,ij,jf->if', filters, envelope, col_feat) / NORM_DIV  32.3 us
  transfers between devices with their start and end apart: 7, of which 7 were waited for; matrix products, arithmetic and copies ran while one was open for 5% of the time, Pallas kernels for 0%

commit v1 on v0

--- a/solution.py
+++ b/solution.py
@@ -1,3 +1,4 @@
+import functools
 from functools import partial
 import math
 import jax
@@ -9,6 +10,19 @@
 CUTOFF = 5.0
 NORM_DIV = 4.0
 HIGH = lax.Precision.HIGHEST
+
+
+def bring_quotas_in(vals, chip_axis):
+    xs_all = []
+    for _ in range(jax.lax.axis_size(chip_axis)):
+        xs_all.append(vals)
+    x_new = jnp.stack(xs_all, axis=0)
+    odd = jax.lax.all_to_all(x_new, chip_axis, 0, 0)
+    prior = jnp.concatenate(odd, axis=0)
+    return prior
+
+
+bring_shifts_all_now = functools.partial(bring_quotas_in, chip_axis="row")
 
 
 def shifted_softplus(values):
@@ -87,7 +101,7 @@
     for layer_idx in range(LAYERS):
         mixed_in = jnp.dot(features, w_in[layer_idx], precision=HIGH)
         col_feats, col_coords = (
-            lax.all_gather(mixed_in, "row", axis=0, tiled=True),
+            bring_shifts_all_now(mixed_in),
             lax.all_gather(positions, "row", axis=1, tiled=True),
         )
         partial_sum = jnp.zeros((n_coldev * block_len, feat_width), jnp.float32)

time: 692 us -> 657 us (0.949)
  blocking collectives: 122 us -> 50.8 us
  starting transfers between devices: 0.91 us -> 15.2 us
  waiting for transfers between devices: 351 us -> 363 us
    all_gather x2 -> x0, blocking collectives: 70.3 us -> none  [body(): lax.all_gather(mixed_in, 'row', axis=0, tiled=True)]
    all_to_all x0 -> x2, starting transfers between devices: none -> 14.5 us  [bring_quotas_in(): odd = jax.lax.all_to_all(x_new, chip_axis, 0, 0)]
    reduce_scatter x2, waiting for transfers between devices: 96.2 us -> 108 us  [body(): lax.psum_scatter(partial_sum, 'col', scatter_dimension=0, tiled=True)]
  transfers between devices with their start and end apart: 7 -> 9, of which waited for: 7 -> 7; matrix products, arithmetic and copies ran while one was open for 5% -> 10% of each run, Pallas kernels for 0% -> 0%
where the time goes in v1:
time: 657 us; the launch traced here: 647 us
  waiting for transfers between devices  363 us (55%)
  matrix products  147 us (22%)
  blocking collectives  50.8 us (8%)
  other arithmetic  37.7 us (6%)
  between operations  18 us (3%)
  starting transfers between devices  15.2 us (2%)
  local copies, waits for them, and re-layouts  14.4 us (2%)
    unnamed x9, waiting for transfers between devices  132 us
    reduce_scatter x2, waiting for transfers between devices, body(): lax.psum_scatter(partial_sum, 'col', scatter_dimension=0, tiled=True)  108 us
    dot_general x8, matrix products, tile_message(): jnp.dot(expand.reshape(rows_here * rows_here, n_gauss), rbf_w, preferred_...  75.4 us
    reduce_scatter x1, waiting for transfers between devices, body(): lax.psum_scatter(grad_colx, 'row', scatter_dimension=0, tiled=True)  71.7 us
    dot_general x8, matrix products, tile_message(): jnp.dot(hidden, filt_w, preferred_element_type=jnp.float32)  62.5 us
    all_gather x2, waiting for transfers between devices, body(): grad_rows = lax.all_gather(grad_msg, 'col', axis=0, tiled=True)  50.7 us
    dot_general x8, other arithmetic, tile_message(): return jnp.einsum('ijf,ij,jf->if', filters, envelope, col_feat) / NORM_DIV  32.3 us
    all_gather x1, blocking collectives, body(): lax.all_gather(positions, 'row', axis=1, tiled=True)  31.3 us
  transfers between devices with their start and end apart: 9, of which 7 were waited for; matrix products, arithmetic and copies ran while one was open for 10% of the time, Pallas kernels for 0%

profile of v1, /device:TPU:0, one launch (start us, length us, event | category | flops | bytes accessed | tf_op | source)
XLA Modules:
  0.0 646.6 jit_solution(7162189615139306238)
XLA Ops:
  10.8 7.9 %all-to-all-start = ((f32[8,128,128]{2,1,0:T(8,128)}), f32[8,128,128]{2,1,0:T(8,128)S(1)}, u32[]{:S(2)}, u32[]{:S(2)}) async-start(f32[8,128,128]{2,1,0:T(8,128)} %stack.4), calls=%async_computation | async-start | bytes 1048576 | tf_op jit(solution)/shard_map/all_to_all | solution.py:20
  22.9 19.5 %all_gather.13 = f32[3,2048]{1,0:T(4,128)S(1)} all-gather(f32[3,128]{1,0:T(4,128)} %param.15), channel_id=1, replica_groups=mesh['row'=8,'col'=16] {'col'}, dimensions={1}, use_global_device_ids=true | all-gather | bytes 26112 | tf_op jit(solution)/shard_map/all_gather | solution.py:95
  42.3 31.3 %all_gather.14 = f32[3,1024]{1,0:T(4,128)S(1)} all-gather(f32[3,128]{1,0:T(4,128)} %param.15), channel_id=1, replica_groups=mesh['row'=8,'col'=16] {'row'}, dimensions={1}, use_global_device_ids=true | all-gather | bytes 13824 | tf_op jit(solution)/shard_map/all_gather | solution.py:105
  78.1 12.2 %add_convert_fusion.3 = (bf16[16384,128]{1,0:T(8,128)(2,1)}, f32[16384,128]{1,0:T(8,128)}) fusion(f32[128]{0:T(128)S(1)} %get-tuple-element.65, bf16[2,256,128]{2,1,0:T(8,128)(2,1)} %param.21, f32[256]{0:T(256)S(1)} %convert_multiply_fusion, f32[16384]{0:T(1024)S(1)} %get-tuple-element.54), kind=kOutput, calls=%fused_computation.93 | convolution fusion | flops 1109393408 | bytes 12715520 | tf_op jit(solution)/shard_map/dot_general | solution.py:42
  90.4 11.4 %add_convert_fusion.2 = (bf16[16384,128]{1,0:T(8,128)(2,1)}, f32[16384,128]{1,0:T(8,128)}) fusion(f32[128]{0:T(128)S(1)} %get-tuple-element.65, bf16[2,256,128]{2,1,0:T(8,128)(2,1)S(1)} %copy-done.24, f32[16384]{0:T(1024)S(1)} %get-tuple-element.59, f32[256]{0:T(256)S(1)} %convert_multiply_fusion), kind=kOutput, calls=%fused_computation.90 | convolution fusion | flops 1109393408 | bytes 12715520 | tf_op jit(solution)/shard_map/dot_general | solution.py:42
  101.8 6.9 %multiply_reduce_fusion.5 = (f32[128,128]{0,1:T(8,128)S(1)}, f32[128,128,128]{2,1,0:T(8,128)}) fusion(f32[128,128]{0,1:T(8,128)S(1)} %get-tuple-element.45, f32[128,128]{1,0:T(8,128)S(1)} %get-tuple-element.53, bf16[128,128,128]{2,1,0:T(8,128)(2,1)} %bitcast.254, bf16[2,128,128]{2,1,0:T(8,128)(2,1)S(1)} %copy-done.13), kind=kOutput, calls=%fused_computation.87 | convolution fusion | flops 543145984 | bytes 12812288 | tf_op jit(solution)/shard_map/dot_general | solution.py:50
  108.8 6.9 %multiply_reduce_fusion.4 = (f32[128,128]{0,1:T(8,128)S(1)}, f32[128,128,128]{2,1,0:T(8,128)}) fusion(f32[128,128]{0,1:T(8,128)S(1)} %get-tuple-element.44, f32[128,128]{1,0:T(8,128)S(1)} %get-tuple-element.52, bf16[128,128,128]{2,1,0:T(8,128)(2,1)} %bitcast.252, bf16[2,128,128]{2,1,0:T(8,128)(2,1)S(1)} %copy-done.13), kind=kOutput, calls=%fused_computation.86 | convolution fusion | flops 543145984 | bytes 12812288 | tf_op jit(solution)/shard_map/dot_general | solution.py:50
  117.1 11.6 %add_convert_fusion.1 = (bf16[16384,128]{1,0:T(8,128)(2,1)}, f32[16384,128]{1,0:T(8,128)}) fusion(f32[128]{0:T(128)S(1)} %get-tuple-element.64, bf16[2,256,128]{2,1,0:T(8,128)(2,1)S(1)} %copy-done.24, f32[256]{0:T(256)S(1)} %convert_multiply_fusion, f32[16384]{0:T(1024)S(1)} %get-tuple-element.54), kind=kOutput, calls=%fused_computation.89 | convolution fusion | flops 1109393408 | bytes 12715520 | tf_op jit(solution)/shard_map/dot_general | solution.py:42
  128.7 47.3 %reduce-scatter.10.cloned.1.call-done = f32[128,128]{0,1:T(8,128)} async-done(((f32[2048,128]{0,1:T(8,128)}), f32[128,128]{0,1:T(8,128)}) %reduce-scatter.10.cloned.1.call-update) | async-done | bytes 65552 | tf_op jit(solution)/shard_map/reduce_scatter | solution.py:124
  178.4 6.6 %all-to-all-start.1 = ((f32[8,128,128]{2,1,0:T(8,128)}), f32[8,128,128]{2,1,0:T(8,128)S(1)}, u32[]{:S(2)}, u32[]{:S(2)}) async-start(f32[8,128,128]{2,1,0:T(8,128)} %stack.5), calls=%async_computation.2 | async-start | bytes 1048576 | tf_op jit(solution)/shard_map/all_to_all | solution.py:20
  185.1 11.4 %add_convert_fusion = (bf16[16384,128]{1,0:T(8,128)(2,1)}, f32[16384,128]{1,0:T(8,128)}) fusion(f32[128]{0:T(128)S(1)} %get-tuple-element.64, bf16[2,256,128]{2,1,0:T(8,128)(2,1)S(1)} %copy-done.24, f32[16384]{0:T(1024)S(1)} %get-tuple-element.59, f32[256]{0:T(256)S(1)} %convert_multiply_fusion), kind=kOutput, calls=%fused_computation.88 | convolution fusion | flops 1109393408 | bytes 12715520 | tf_op jit(solution)/shard_map/dot_general | solution.py:42
  196.4 6.9 %multiply_reduce_fusion.3 = (f32[128,128]{0,1:T(8,128)S(1)}, f32[128,128,128]{2,1,0:T(8,128)}) fusion(f32[128,128]{0,1:T(8,128)S(1)} %get-tuple-element.43, f32[128,128]{1,0:T(8,128)S(1)} %get-tuple-element.53, bf16[128,128,128]{2,1,0:T(8,128)(2,1)} %bitcast.251, bf16[2,128,128]{2,1,0:T(8,128)(2,1)S(1)} %copy-done.13), kind=kOutput, calls=%fused_computation.85 | convolution fusion | flops 543145984 | bytes 12812288 | tf_op jit(solution)/shard_map/dot_general | solution.py:50
  203.4 6.9 %multiply_reduce_fusion.2 = (f32[128,128]{0,1:T(8,128)S(1)}, f32[128,128,128]{2,1,0:T(8,128)}) fusion(f32[128,128]{0,1:T(8,128)S(1)} %get-tuple-element.42, f32[128,128]{1,0:T(8,128)S(1)} %get-tuple-element.52, bf16[128,128,128]{2,1,0:T(8,128)(2,1)} %bitcast.253, bf16[2,128,128]{2,1,0:T(8,128)(2,1)S(1)} %copy-done.13), kind=kOutput, calls=%fused_computation.84 | convolution fusion | flops 543145984 | bytes 12812288 | tf_op jit(solution)/shard_map/dot_general | solution.py:50
  212.1 61.2 %reduce-scatter.12.cloned.1.call-done = f32[128,128]{0,1:T(8,128)} async-done(((f32[2048,128]{0,1:T(8,128)}), f32[128,128]{0,1:T(8,128)}) %reduce-scatter.12.cloned.1.call-update) | async-done | bytes 65552 | tf_op jit(solution)/shard_map/reduce_scatter | solution.py:124
  276.5 30.8 %all-gather.3.cloned.1.call-done = f32[2048,128]{1,0:T(8,128)} async-done(((f32[128,128]{1,0:T(8,128)}), f32[2048,128]{1,0:T(8,128)}) %all-gather.3.cloned.1.call-update) | async-done | bytes 1048592 | tf_op jit(solution)/shard_map/all_gather | solution.py:140
  308.1 5.2 multiply_reduce_fusion
  313.4 5.2 multiply_reduce_fusion.1
  319.6 71.7 %reduce-scatter.14.cloned.1.call-done = f32[128,128]{1,0:T(8,128)} async-done(((f32[1024,128]{1,0:T(8,128)}), f32[128,128]{1,0:T(8,128)}) %reduce-scatter.14.cloned.1.call-update) | async-done | bytes 65552 | tf_op jit(solution)/shard_map/reduce_scatter | solution.py:163
  393.6 5.6 fusion.49
  399.2 5.7 fusion.48
  404.9 19.9 %all-gather.5.cloned.1.call-done = f32[2048,128]{1,0:T(8,128)} async-done(((f32[128,128]{1,0:T(8,128)}), f32[2048,128]{1,0:T(8,128)}) %all-gather.5.cloned.1.call-update) | async-done | bytes 1048592 | tf_op jit(solution)/shard_map/all_gather | solution.py:140
  425.7 3.1 bitcast_multiply_fusion.6
  428.8 9.3 %fusion.17 = bf16[16384,128]{1,0:T(8,128)(2,1)S(1)} fusion(bf16[16384,128]{1,0:T(8,128)(2,1)S(1)} %bitcast.258, f32[16384,128]{1,0:T(8,128)} %get-tuple-element.79, bf16[2,128,128]{2,1,0:T(8,128)(2,1)S(1)} %copy-done.13), kind=kOutput, calls=%fused_computation.45 | convolution fusion | flops 566231040 | bytes 16809984 | tf_op jit(solution)/shard_map/transpose(jvp())/dot_general | solution.py:50
  438.1 7.1 %fusion.26 = f32[16384]{0:T(1024)S(1)} fusion(f32[256]{0:T(256)S(1)} %convert_multiply_fusion, f32[16384]{0:T(1024)S(1)} %get-tuple-element.54, bf16[16384,128]{1,0:T(8,128)(2,1)S(1)} %fusion.17, bf16[2,256,128]{2,1,0:T(8,128)(2,1)S(1)} %copy-done.24), kind=kOutput, calls=%fused_computation.54 | convolution fusion | flops 1111474176 | bytes 4391936 | tf_op jit(solution)/shard_map/transpose(jvp())/dot_general | solution.py:42
  445.3 7.1 %fusion.21 = bf16[16384,128]{1,0:T(8,128)(2,1)S(1)} fusion(bf16[16384,128]{1,0:T(8,128)(2,1)S(1)} %bitcast.256, f32[16384,128]{1,0:T(8,128)S(1)} %bitcast.268, bf16[2,128,128]{2,1,0:T(8,128)(2,1)S(1)} %copy-done.13), kind=kOutput, calls=%fused_computation.49 | convolution fusion | flops 566231040 | bytes 16809984 | tf_op jit(solution)/shard_map/transpose(jvp())/dot_general | solution.py:50
  452.4 7.3 %fusion.27 = f32[16384]{0:T(1024)S(1)} fusion(f32[256]{0:T(256)S(1)} %convert_multiply_fusion, f32[16384]{0:T(1024)S(1)} %get-tuple-element.54, bf16[16384,128]{1,0:T(8,128)(2,1)S(1)} %fusion.21, bf16[2,256,128]{2,1,0:T(8,128)(2,1)S(1)} %copy-done.24), kind=kOutput, calls=%fused_computation.55 | convolution fusion | flops 1111474176 | bytes 4391936 | tf_op jit(solution)/shard_map/transpose(jvp())/dot_general | solution.py:42
  467.3 9.2 %fusion.23 = bf16[16384,128]{1,0:T(8,128)(2,1)S(1)} fusion(bf16[16384,128]{1,0:T(8,128)(2,1)S(1)} %bitcast.257, f32[16384,128]{1,0:T(8,128)} %get-tuple-element.75, bf16[2,128,128]{2,1,0:T(8,128)(2,1)S(1)} %copy-done.13), kind=kOutput, calls=%fused_computation.51 | convolution fusion | flops 566231040 | bytes 16809984 | tf_op jit(solution)/shard_map/transpose(jvp())/dot_general | solution.py:50
  476.5 7.3 %fusion.25 = f32[16384]{0:T(1024)S(1)} fusion(f32[16384]{0:T(1024)S(1)} %get-tuple-element.59, f32[256]{0:T(256)S(1)} %convert_multiply_fusion, bf16[16384,128]{1,0:T(8,128)(2,1)S(1)} %fusion.23, bf16[2,256,128]{2,1,0:T(8,128)(2,1)S(1)} %copy-done.24), kind=kOutput, calls=%fused_computation.53 | convolution fusion | flops 1111474176 | bytes 4391936 | tf_op jit(solution)/shard_map/transpose(jvp())/dot_general | solution.py:42
  483.8 9.2 %fusion.19 = bf16[16384,128]{1,0:T(8,128)(2,1)S(1)} fusion(bf16[16384,128]{1,0:T(8,128)(2,1)S(1)} %bitcast.255, f32[16384,128]{1,0:T(8,128)} %get-tuple-element.83, bf16[2,128,128]{2,1,0:T(8,128)(2,1)S(1)} %copy-done.13), kind=kOutput, calls=%fused_computation.47 | convolution fusion | flops 566231040 | bytes 16809984 | tf_op jit(solution)/shard_map/transpose(jvp())/dot_general | solution.py:50
  493.1 7.1 %fusion.24 = f32[16384]{0:T(1024)S(1)} fusion(f32[16384]{0:T(1024)S(1)} %get-tuple-element.59, f32[256]{0:T(256)S(1)} %convert_multiply_fusion, bf16[16384,128]{1,0:T(8,128)(2,1)S(1)} %fusion.19, bf16[2,256,128]{2,1,0:T(8,128)(2,1)S(1)} %copy-done.24), kind=kOutput, calls=%fused_computation.52 | convolution fusion | flops 1111474176 | bytes 4391936 | tf_op jit(solution)/shard_map/transpose(jvp())/dot_general | solution.py:42
  504.7 69.4 %reduce-scatter.18.cloned.1.call-done = f32[128,3]{1,0:T(8,128)} async-done(((f32[1024,3]{1,0:T(8,128)}), f32[128,3]{1,0:T(8,128)}) %reduce-scatter.18.cloned.1.call-update) | async-done | bytes 1552
  575.1 62.7 %reduce-scatter.16.cloned.1.call-done = f32[128,3]{1,0:T(8,128)} async-done(((f32[2048,3]{1,0:T(8,128)}), f32[128,3]{1,0:T(8,128)}) %reduce-scatter.16.cloned.1.call-update) | async-done | bytes 1552
  (149 shorter events, 37.6 us)
Async XLA Ops:
  10.8 91.0 %all-to-all-start = ((f32[8,128,128]{2,1,0:T(8,128)}), f32[8,128,128]{2,1,0:T(8,128)S(1)}, u32[]{:S(2)}, u32[]{:S(2)}) async-start(f32[8,128,128]{2,1,0:T(8,128)} %stack.4), calls=%async_computation | async-start | bytes 1048576 | tf_op jit(solution)/shard_map/all_to_all | solution.py:20
  18.7 157.3 %reduce-scatter.10.cloned.1.call-start = ((), (), s32[]{:S(2)}) async-start(), calls=%async_computation.7 | async-start | bytes 1114112 | tf_op jit(solution)/shard_map/reduce_scatter | solution.py:124
  75.3 15.1 %copy-start.16 = (f32[3,128]{1,0:T(4,128)}, f32[3,128]{1,0:T(4,128)S(1)}, u32[]{:S(2)}) copy-start(f32[3,128]{1,0:T(4,128)S(1)} %get-tuple-element.60) | copy-start | bytes 4612
  75.3 15.0 %copy-start.18 = (f32[3,128]{1,0:T(4,128)}, f32[3,128]{1,0:T(4,128)S(1)}, u32[]{:S(2)}) copy-start(f32[3,128]{1,0:T(4,128)S(1)} %get-tuple-element.62) | copy-start | bytes 4612
  75.3 15.0 %copy-start.22 = (f32[3,128]{1,0:T(4,128)}, f32[3,128]{1,0:T(4,128)S(1)}, u32[]{:S(2)}) copy-start(f32[3,128]{1,0:T(4,128)S(1)} %get-tuple-element.63) | copy-start | bytes 4612
  75.4 14.9 %copy-start.7 = (f32[128,128]{1,0:T(8,128)}, f32[128,128]{1,0:T(8,128)S(1)}, u32[]{:S(2)}) copy-start(f32[128,128]{1,0:T(8,128)S(1)} %fusion.74) | copy-start | bytes 196612
  76.0 14.4 %copy-start.9 = (f32[128,128]{1,0:T(8,128)}, f32[128,128]{1,0:T(8,128)S(1)}, u32[]{:S(2)}) copy-start(f32[128,128]{1,0:T(8,128)S(1)} %fusion.75) | copy-start | bytes 196612
  78.1 12.2 %copy-start.24 = (bf16[2,256,128]{2,1,0:T(8,128)(2,1)S(1)}, bf16[2,256,128]{2,1,0:T(8,128)(2,1)}, u32[]{:S(2)}) copy-start(bf16[2,256,128]{2,1,0:T(8,128)(2,1)} %param.21) | copy-start | bytes 393220
  90.4 11.4 %copy-start.13 = (bf16[2,128,128]{2,1,0:T(8,128)(2,1)S(1)}, bf16[2,128,128]{2,1,0:T(8,128)(2,1)}, u32[]{:S(2)}) copy-start(bf16[2,128,128]{2,1,0:T(8,128)(2,1)} %param.23) | copy-start | bytes 196612
  117.0 59.0 %copy-start.11 = (f32[2,128,128]{2,1,0:T(8,128)S(1)}, f32[2,128,128]{2,1,0:T(8,128)}, u32[]{:S(2)}) copy-start(f32[2,128,128]{2,1,0:T(8,128)} %param.24) | copy-start | bytes 393220
  117.0 60.1 %copy-start.14 = (f32[2,128,128]{2,1,0:T(8,128)S(1)}, f32[2,128,128]{2,1,0:T(8,128)}, u32[]{:S(2)}) copy-start(f32[2,128,128]{2,1,0:T(8,128)} %param.25) | copy-start | bytes 393220
  117.0 60.3 %copy-start.12 = (f32[2,128,128]{2,1,0:T(8,128)S(1)}, f32[2,128,128]{2,1,0:T(8,128)}, u32[]{:S(2)}) copy-start(f32[2,128,128]{2,1,0:T(8,128)} %param.20) | copy-start | bytes 393220
  178.4 18.0 %all-to-all-start.1 = ((f32[8,128,128]{2,1,0:T(8,128)}), f32[8,128,128]{2,1,0:T(8,128)S(1)}, u32[]{:S(2)}, u32[]{:S(2)}) async-start(f32[8,128,128]{2,1,0:T(8,128)} %stack.5), calls=%async_computation.2 | async-start | bytes 1048576 | tf_op jit(solution)/shard_map/all_to_all | solution.py:20
  185.0 88.2 %reduce-scatter.12.cloned.1.call-start = ((), (), s32[]{:S(2)}) async-start(), calls=%async_computation.8 | async-start | bytes 1114112 | tf_op jit(solution)/shard_map/reduce_scatter | solution.py:124
  203.3 71.3 %copy-start.15 = (f32[128,64]{0,1:T(8,128)S(1)}, f32[128,64]{0,1:T(8,128)}, u32[]{:S(2)}) copy-start(f32[128,64]{0,1:T(8,128)} %param.26) | copy-start | bytes 98308
  203.3 71.5 %copy-start.25 = (f32[64]{0:T(128)S(1)}, f32[64]{0:T(128)}, u32[]{:S(2)}) copy-start(f32[64]{0:T(128)} %param.27) | copy-start | bytes 772
  211.6 95.7 %all-gather.3.cloned.1.call-start = ((), (), s32[]{:S(2)}) async-start(), calls=%async_computation.9 | async-start | bytes 1114112 | tf_op jit(solution)/shard_map/all_gather | solution.py:140
  276.4 114.8 %reduce-scatter.14.cloned.1.call-start = ((), (), s32[]{:S(2)}) async-start(), calls=%async_computation.10 | async-start | bytes 589824 | tf_op jit(solution)/shard_map/reduce_scatter | solution.py:163
  319.5 105.3 %all-gather.5.cloned.1.call-start = ((), (), s32[]{:S(2)}) async-start(), calls=%async_computation.11 | async-start | bytes 1114112 | tf_op jit(solution)/shard_map/all_gather | solution.py:140
  393.5 180.6 %reduce-scatter.18.cloned.1.call-start = ((), (), s32[]{:S(2)}) async-start(), calls=%async_computation.13 | async-start | bytes 589824
  425.7 19.5 %slice-start.4 = ((s8[8388608]{0:T(1024)(128)(4,1)}), s8[4194304]{0:T(1024)(128)(4,1)S(1)}, s32[]{:S(2)}) async-start(s8[8388608]{0:T(1024)(128)(4,1)} %bitcast.267), calls=%async_computation.18 | async-start | bytes 8388608
  428.8 16.5 %slice-start.5 = ((s8[8388608]{0:T(1024)(128)(4,1)}), s8[4194304]{0:T(1024)(128)(4,1)S(1)}, s32[]{:S(2)}) async-start(s8[8388608]{0:T(1024)(128)(4,1)} %bitcast.267), calls=%async_computation.19 | async-start | bytes 8388608
  438.1 21.6 %slice-start.2 = ((s8[8388608]{0:T(1024)(128)(4,1)}), s8[4194304]{0:T(1024)(128)(4,1)S(1)}, s32[]{:S(2)}) async-start(s8[8388608]{0:T(1024)(128)(4,1)} %bitcast.249), calls=%async_computation.16 | async-start | bytes 8388608
  445.2 14.5 %slice-start.3 = ((s8[8388608]{0:T(1024)(128)(4,1)}), s8[4194304]{0:T(1024)(128)(4,1)S(1)}, s32[]{:S(2)}) async-start(s8[8388608]{0:T(1024)(128)(4,1)} %bitcast.249), calls=%async_computation.17 | async-start | bytes 8388608
  493.0 7.2 %copy-start.6 = (s32[2,128,128]{2,1,0:T(8,128)S(1)}, s32[2,128,128]{2,1,0:T(8,128)}, u32[]{:S(2)}) copy-start(s32[2,128,128]{2,1,0:T(8,128)} %copy-done.5) | copy-start | bytes 393220
  493.0 7.2 %copy-start.8 = (f32[128,128]{1,0:T(8,128)S(1)}, f32[128,128]{1,0:T(8,128)}, u32[]{:S(2)}) copy-start(f32[128,128]{1,0:T(8,128)} %copy-done.7) | copy-start | bytes 196612
  493.0 7.7 %copy-start.21 = (f32[3,128]{1,0:T(4,128)S(1)}, f32[3,128]{1,0:T(4,128)}, u32[]{:S(2)}) copy-start(f32[3,128]{1,0:T(4,128)} %copy-done.20) | copy-start | bytes 4612
  493.0 7.7 %copy-start.23 = (f32[3,128]{1,0:T(4,128)S(1)}, f32[3,128]{1,0:T(4,128)}, u32[]{:S(2)}) copy-start(f32[3,128]{1,0:T(4,128)} %copy-done.22) | copy-start | bytes 4612
  493.0 8.1 %copy-start.17 = (f32[3,128]{1,0:T(4,128)S(1)}, f32[3,128]{1,0:T(4,128)}, u32[]{:S(2)}) copy-start(f32[3,128]{1,0:T(4,128)} %copy-done.16) | copy-start | bytes 4612
  493.1 8.1 %copy-start.19 = (f32[3,128]{1,0:T(4,128)S(1)}, f32[3,128]{1,0:T(4,128)}, u32[]{:S(2)}) copy-start(f32[3,128]{1,0:T(4,128)} %copy-done.18) | copy-start | bytes 4612
  493.1 146.2 %copy-start.1 = (f32[100,128]{1,0:T(8,128)S(1)}, f32[100,128]{1,0:T(8,128)}, u32[]{:S(2)}) copy-start(f32[100,128]{1,0:T(8,128)} %param.19) | copy-start | bytes 153604
  502.5 135.3 %reduce-scatter.16.cloned.1.call-start = ((), (), s32[]{:S(2)}) async-start(), calls=%async_computation.12 | async-start | bytes 1114112
  (9 other events, 20.1 us)
Sparse Core Ops, SparseCore 0:
  117.1 58.7 reduce-scatter.9
  211.7 61.4 reduce-scatter.11
  276.5 30.6 all-gather.2
  319.6 71.5 reduce-scatter.13
  393.7 31.0 all-gather.4
  502.6 71.4 reduce-scatter.17
  576.5 61.2 reduce-scatter.15
